TPU v7x, 256 devices: a whole 4x4x8 slice. The times are simulated.
256 devices in a mesh: tm: 64 (over z_hi, y, x), freq: 4 (over z_lo, core).
Axes of the slice: x: 4, y: 4, z: 8 (z_hi: 4, z_lo: 2; z = z_hi * 2 + z_lo), core: 2. Of those that a mesh axis runs over, the one named last changes fastest.
Arguments:
- spectrum: bfloat16 [1024, 49152], P('freq', 'tm'), may hold values from 0.0099487305 to 10
- decay_rate: float32 [1024], P('freq'), may hold values from 1e-07 to 0.03
- init_state: float32 [1024], P('freq'), may hold values from 0.3 to 3
- clip_ids: int32 [49152], P('tm'), may hold values from 0 to 5, never falling along the last dimension, each value on 1 to 16384 neighbouring positions
- encoder: bfloat16 [256, 1024], P(None, 'freq'), may hold values from -0.1875 to 0.1875
- gauss_noise: float32 [256, 49152], P(None, 'tm'), may hold values from -3 to 3
- uniform_noise: float32 [2, 256, 49152], P(None, None, 'tm'), may hold values from 0.02 to 1
- boost_count: int32 [256], replicated, may hold values from 1 to 2
- templates: bfloat16 [1024, 4096], P('freq'), may hold values from 0.0099487305 to 1
Outputs:
- frame_loss: float32 [49152], P('tm')
- template_grad: float32 [4096, 1024], P('tm', 'freq')
Inputs may be any that keep to these rules, and one draw needn't show every extreme that they name: `clip_ids`: clip numbers never fall along the frames; each clip holds 1 to 16384 frames, one exactly that many.
All inputs are finite; a program needn't handle non-finite values.
Results may differ from a plain program's by a relative error of at most 0.00033.
Values may be sent and summed in bfloat16 or wider, within the bound.
A program may use at most 64 MiB of HBM per device.

v0:
```python
import jax
import jax.numpy as jnp
from jax import lax
from jax.sharding import PartitionSpec as P

F = 1024
K = 256
L = 16


def prefix(part, axis, combine, identity):
    place = lax.axis_index(axis)
    gathered = jax.tree.map(lambda a: lax.all_gather(a, axis), part)
    state = jax.tree.map(lambda a, e: jnp.zeros_like(a) + jnp.asarray(e, a.dtype), part, identity)

    def one(lap, state):
        return combine(
            state, jax.tree.map(lambda a: lax.dynamic_index_in_dim(a, lap, 0, False), gathered)
        )

    return lax.fori_loop(0, place, one, state)


def passed_along(value, axis, steps):
    count = lax.axis_size(axis)
    leading, last = (max(0, -steps), min(count, count - steps))
    return lax.ppermute(value, axis, [(source, source + steps) for source in range(leading, last)])


def compose(former, latter):
    return (former[0] * latter[0], latter[0] * former[1] + latter[1])


def linked(former, latter):
    p_one, q_one, first_one, last_one, start_one, mark_one = former
    p_two, q_two, first_two, last_two, start_two, mark_two = latter
    joined = (last_one >= 0.0) & (first_two >= 0.0) & (first_two != last_one)
    factor = jnp.where(joined, 0.8, 1.0)
    scaled = p_two * factor
    merged_p = scaled * p_one
    merged_q = scaled * q_one + q_two
    first_clip = jnp.where(first_one >= 0.0, first_one, first_two)
    start_frame = jnp.where(first_one >= 0.0, start_one, start_two)
    last_clip = jnp.where(last_two >= 0.0, last_two, last_one)
    latest = jnp.maximum(jnp.maximum(mark_one, jnp.where(joined, start_two, -1.0)), mark_two)
    return (merged_p, merged_q, first_clip, last_clip, start_frame, latest)


def topic_mixture(logits, gaussian, uniforms, boost_count):
    concentration = jax.nn.softplus(logits) + 0.5
    boosted = boost_count[:, None]
    shape_total = concentration + boosted.astype(jnp.float32)
    offset = shape_total - 1.0 / 3.0
    spread = lax.rsqrt(9.0 * offset)
    linear = 1.0 + spread * gaussian
    gamma_draw = offset * linear * linear * linear * jnp.exp(jnp.log(uniforms[0]) / concentration)
    gamma_draw = gamma_draw * jnp.where(
        boosted >= 2, jnp.exp(jnp.log(uniforms[1]) / (concentration + 1.0)), 1.0
    )
    return (gamma_draw / jnp.sum(gamma_draw, axis=0, keepdims=True)).astype(jnp.bfloat16)


def on_device(
    spectrum,
    decay_rate,
    init_state,
    clip_ids,
    encoder,
    gauss_noise,
    uniform_noise,
    boost_count,
    templates,
):
    frames = spectrum.shape[1]
    bins = spectrum.shape[0]
    rim_width = L - 1
    spectral = spectrum.astype(jnp.float32)
    changed = clip_ids[1:] != clip_ids[:-1]
    factor_row = jnp.concatenate(
        [jnp.ones((1,), jnp.float32), jnp.where(changed, 0.8, 1.0).astype(jnp.float32)]
    )
    rates = (1.0 - decay_rate)[:, None] * factor_row[None, :]
    inputs = decay_rate[:, None] * spectral
    running, summed = lax.associative_scan(compose, (rates, inputs), axis=1)
    anchor = lax.axis_index("tm") * frames
    positions = anchor + jnp.arange(frames, dtype=jnp.int32)
    marks = jnp.where(jnp.concatenate([jnp.zeros((1,), bool), changed]), positions, -1)
    clip_float = clip_ids.astype(jnp.float32)
    summary = (
        running[:, -1],
        summed[:, -1],
        clip_float[:1],
        clip_float[-1:],
        jnp.reshape(anchor.astype(jnp.float32), (1,)),
        jnp.reshape(jnp.max(marks).astype(jnp.float32), (1,)),
    )
    minus_one = jnp.full((1,), -1.0, jnp.float32)
    identity_tuple = (
        jnp.ones((bins,), jnp.float32),
        jnp.zeros((bins,), jnp.float32),
        minus_one,
        minus_one,
        minus_one,
        minus_one,
    )
    before = prefix(summary, "tm", linked, identity_tuple)
    junction = (before[3] >= 0.0) & (clip_float[:1] != before[3])
    entry = jnp.where(junction, 0.8, 1.0) * (before[0] * init_state + before[1])
    smooth = running * entry[:, None] + summed
    normed = (spectral * lax.rsqrt(smooth + 0.1)).astype(jnp.bfloat16)
    code_part = jnp.dot(encoder, normed, preferred_element_type=jnp.float32)
    logits = lax.psum(code_part, "freq")
    proportions = topic_mixture(logits, gauss_noise, uniform_noise, boost_count)
    topics = proportions.shape[0]
    rim = passed_along(proportions[:, frames - rim_width :], "tm", 1)
    extended = jnp.concatenate([rim, proportions], axis=1)
    flags = jnp.concatenate([junction, changed]).astype(jnp.int32)
    clean = jnp.cumsum(flags) == 0
    clip_pad = jnp.concatenate([jnp.full((rim_width,), -1, jnp.int32), clip_ids])
    lag_rows = []
    mask_rows = []
    for lag in range(L):
        begin = rim_width - lag
        lag_rows.append(extended[:, begin : begin + frames])
        source = jnp.arange(frames, dtype=jnp.int32) - lag
        same_clip = clip_pad[begin : begin + frames] == clip_ids
        earlier = clean & (before[5] <= (anchor + source).astype(jnp.float32))
        mask_rows.append(jnp.where(source >= 0, same_clip, earlier))
    valid = jnp.stack(mask_rows).astype(jnp.bfloat16)
    stacked = (jnp.stack(lag_rows, axis=1) * valid[None]).reshape(topics * L, frames)
    recon = jnp.dot(templates, stacked, preferred_element_type=jnp.float32)
    sums_part = (
        jnp.sum(recon, axis=0),
        jnp.sum(spectral, axis=0),
        jnp.sum(spectral * jnp.log(recon), axis=0),
    )
    recon_sum, spec_sum, log_sum = lax.psum((sums_part[0], sums_part[1], sums_part[2]), "freq")
    frame_loss = jnp.log(recon_sum) - log_sum / spec_sum
    scale_factor = F * K / (frames * lax.axis_size("tm"))
    ratio = (
        scale_factor * (1.0 / recon_sum[None, :] - spectral / (spec_sum[None, :] * recon))
    ).astype(jnp.bfloat16)
    owned_rows = topics * L // lax.axis_size("tm")
    full_grad = lax.dot_general(
        stacked, ratio, (((1,), (1,)), ((), ())), preferred_element_type=jnp.float32
    )
    total_grad = lax.psum(full_grad, "tm")
    template_grad = lax.dynamic_slice_in_dim(
        total_grad, lax.axis_index("tm") * owned_rows, owned_rows, 0
    )
    return (frame_loss, template_grad)


def solution(mesh):
    placed = (
        P("freq", "tm"),
        P("freq"),
        P("freq"),
        P("tm"),
        P(None, "freq"),
        P(None, "tm"),
        P(None, None, "tm"),
        P(),
        P("freq", None),
    )
    return jax.shard_map(
        on_device, mesh=mesh, in_specs=placed, out_specs=(P("tm"), P("tm", "freq")), check_vma=False
    )
```

profile of v0, /device:TPU:2, one launch (start us, length us, event | category | flops | bytes accessed | tf_op | source)
XLA Modules:
  0.0 1997.8 jit_solution(15807336264710183670)
XLA Ops:
  17.0 3.1 slice.440
  20.2 3.2 slice.439
  23.3 2.3 fusion.127
  98.1 3.2 slice.480
  121.8 2.5 pad.144
  133.7 2.9 pad.128
  137.3 187.8 %all-gather = f32[16384,1]{0,1:T(1,128)S(1)} all-gather(f32[256,1]{0,1:T(1,128)S(1)} %slice_add_fusion.3), channel_id=2, replica_groups=mesh['tm'=64,'freq'=4] {'tm'}, dimensions={0}, use_global_device_ids=true | all-gather | bytes 66560 | tf_op jit(solution)/shard_map/all_gather | solution.py:13
  335.1 2.9 pad.145
  337.9 2.8 pad.146
  341.5 191.4 %all-gather.2 = f32[16384,1]{0,1:T(1,128)S(1)} all-gather(f32[256,1]{0,1:T(1,128)S(1)} %slice_add_fusion), channel_id=4, replica_groups=mesh['tm'=64,'freq'=4] {'tm'}, dimensions={0}, use_global_device_ids=true | all-gather | bytes 66560 | tf_op jit(solution)/shard_map/all_gather | solution.py:13
  535.8 186.1 %all-reduce.41 = (f32[64]{0:T(128)S(1)}, f32[64]{0:T(128)S(1)}, f32[64]{0:T(128)S(1)}, f32[64]{0:T(128)S(1)}) all-reduce(f32[64]{0:T(128)S(1)} %get-tuple-element.234, f32[64]{0:T(128)} %copy-done.6, f32[64]{0:T(128)S(1)} %dynamic-update-slice.2, f32[64]{0:T(128)S(1)} %dynamic-update-slice.3), channel_id=3, replica_groups=mesh['tm'=64,'freq'=4] {'tm'}, use_global_device_ids=true, to_apply=%add.37 | all-reduce | flops 256 | bytes 2048
  722.0 6.6 while.20
  729.9 3.0 convolution_bitcast_fusion
  733.0 2.3 fusion.126
  735.3 2.3 copy.87
  740.8 435.0 %all-reduce.46.cloned.1.call-done = f32[256,768]{0,1:T(8,128)} async-done(((f32[256,768]{0,1:T(8,128)}), f32[256,768]{0,1:T(8,128)}) %all-reduce.46.cloned.1.call-update) | async-done | bytes 786448 | tf_op jit(solution)/shard_map/psum | solution.py:112
  1175.8 2.8 fusion.124
  1179.5 3.5 collective-permute-start
  1197.7 7.2 broadcast_multiply_fusion
  1204.9 9.0 copy.83
  1213.9 5.5 fusion.136
  1221.1 10.1 all-reduce.42
  1231.9 6.8 fusion.11
  1238.7 750.8 %all-reduce.48.cloned.1.call-done = f32[4096,256]{1,0:T(8,128)} async-done(((f32[4096,256]{1,0:T(8,128)}), f32[4096,256]{1,0:T(8,128)}) %all-reduce.48.cloned.1.call-update) | async-done | bytes 4194320 | tf_op jit(solution)/shard_map/psum | solution.py:147
  (242 shorter events, 151.2 us)
Async XLA Ops:
  7.2 1206.8 %copy-start = (bf16[256,4096]{1,0:T(8,128)(2,1)S(1)}, bf16[256,4096]{1,0:T(8,128)(2,1)}, u32[]{:S(2)}) copy-start(bf16[256,4096]{1,0:T(8,128)(2,1)} %param.19) | copy-start | bytes 6291460
  7.2 1168.6 %all-reduce.46.cloned.1.call-start = ((), (), s32[]{:S(2)}) async-start(), calls=%async_computation | async-start | bytes 1572864 | tf_op jit(solution)/shard_map/psum | solution.py:112
  9.6 92.4 %copy-start.1 = (f32[256,768]{0,1:T(8,128)}, f32[256,768]{0,1:T(8,128)S(1)}, u32[]{:S(2)}) copy-start(f32[256,768]{0,1:T(8,128)S(1)} %broadcast_multiply_fusion.1) | copy-start | bytes 2359300
  15.4 86.6 %copy-start.3 = (s32[768]{0:T(1024)S(1)}, s32[768]{0:T(1024)}, u32[]{:S(2)}) copy-start(s32[768]{0:T(1024)} %param.14) | copy-start | bytes 9220
  113.3 18.5 slice-start
  119.8 212.0 %copy-start.4 = (pred[767]{0:T(1024)(128)(4,1)S(1)}, pred[767]{0:T(1024)(128)(4,1)}, u32[]{:S(2)}) copy-start(pred[767]{0:T(1024)(128)(4,1)} %get-tuple-element.180) | copy-start | bytes 2305
  119.8 213.5 %slice-start.1 = ((f32[256,768]{0,1:T(8,128)}), f32[256,1]{0,1:T(1,128)S(1)}, s32[]{:S(2)}) async-start(f32[256,768]{0,1:T(8,128)} %convert_multiply_fusion.2), calls=%async_computation.3 | async-start | bytes 2048 | tf_op jit(solution)/shard_map/slice | solution.py:84
  128.7 601.2 %copy-start.2 = (bf16[256,256]{1,0:T(8,128)(2,1)S(1)}, bf16[256,256]{1,0:T(8,128)(2,1)}, u32[]{:S(2)}) copy-start(bf16[256,256]{1,0:T(8,128)(2,1)} %param.15) | copy-start | bytes 393220
  331.8 9.0 copy-start.6
  729.9 10.2 copy-start.5
  732.9 1256.6 %all-reduce.48.cloned.1.call-start = ((), (), s32[]{:S(2)}) async-start(), calls=%async_computation.1 | async-start | bytes 8388608 | tf_op jit(solution)/shard_map/psum | solution.py:147
  1179.5 5.5 collective-permute-start
Sparse Core Ops, SparseCore 0:
  733.0 442.7 all-reduce.45
  1238.8 750.6 all-reduce.47
where the time goes:
time: 2010 us; the launch traced here: 2000 us
  waiting for transfers between devices  1190 us (59%)
  blocking collectives  575 us (29%)
  local copies, waits for them, and re-layouts  126 us (6%)
  other arithmetic  70.4 us (4%)
    psum x1, waiting for transfers between devices, on_device(): total_grad = lax.psum(full_grad, 'tm')  751 us
    psum x1, waiting for transfers between devices, on_device(): logits = lax.psum(code_part, 'freq')  435 us
    all_gather x2, blocking collectives, prefix(): gathered = jax.tree.map(lambda a: lax.all_gather(a, axis), part)  379 us
    unnamed x1, blocking collectives  186 us
    slice x66, local copies, waits for them, and re-layouts, on_device(): running, summed = lax.associative_scan(compose, (rates, inputs), axis=1)  77.9 us
  transfers between devices with their start and end apart: 3, of which 3 were waited for; matrix products, arithmetic and copies ran while one was open for 0% of the time, Pallas kernels for 0%

commit v1 on v0

--- a/solution.py
+++ b/solution.py
@@ -6,6 +6,12 @@
 F = 1024
 K = 256
 L = 16
+
+
+def gather_and_add(x, mesh_axis):
+    parts = lax.all_gather(x, mesh_axis, axis=0, tiled=False)
+    total = parts.sum(axis=0)
+    return total
 
 
 def prefix(part, axis, combine, identity):
@@ -109,7 +115,7 @@
     smooth = running * entry[:, None] + summed
     normed = (spectral * lax.rsqrt(smooth + 0.1)).astype(jnp.bfloat16)
     code_part = jnp.dot(encoder, normed, preferred_element_type=jnp.float32)
-    logits = lax.psum(code_part, "freq")
+    logits = gather_and_add(code_part, "freq")
     proportions = topic_mixture(logits, gauss_noise, uniform_noise, boost_count)
     topics = proportions.shape[0]
     rim = passed_along(proportions[:, frames - rim_width :], "tm", 1)

time: 2010 us -> 1920 us (0.955)
  waiting for transfers between devices: 1190 us -> 1100 us
    psum x1 -> x0, waiting for transfers between devices: 435 us -> none  [on_device(): logits = lax.psum(code_part, 'freq')]
    all_gather x0 -> x1, waiting for transfers between devices: none -> 342 us  [gather_and_add(): parts = lax.all_gather(x, mesh_axis, axis=0, tiled=False)]
  transfers between devices with their start and end apart: 3 -> 3, of which waited for: 3 -> 3; matrix products, arithmetic and copies ran while one was open for 0% -> 1% of each run, Pallas kernels for 0% -> 0%
where the time goes in v1:
time: 1920 us; the launch traced here: 1910 us
  waiting for transfers between devices  1100 us (57%)
  blocking collectives  575 us (30%)
  local copies, waits for them, and re-layouts  127 us (7%)
  other arithmetic  73.5 us (4%)
    psum x1, waiting for transfers between devices, on_device(): total_grad = lax.psum(full_grad, 'tm')  751 us
    all_gather x2, blocking collectives, prefix(): gathered = jax.tree.map(lambda a: lax.all_gather(a, axis), part)  379 us
    all_gather x1, waiting for transfers between devices, gather_and_add(): parts = lax.all_gather(x, mesh_axis, axis=0, tiled=False)  342 us
    unnamed x1, blocking collectives  186 us
    slice x66, local copies, waits for them, and re-layouts, on_device(): running, summed = lax.associative_scan(compose, (rates, inputs), axis=1)  71.4 us
  transfers between devices with their start and end apart: 3, of which 3 were waited for; matrix products, arithmetic and copies ran while one was open for 1% of the time, Pallas kernels for 0%

profile of v1, /device:TPU:2, one launch (start us, length us, event | category | flops | bytes accessed | tf_op | source)
XLA Modules:
  0.0 1910.1 jit_solution(15880466620702573484)
XLA Ops:
  17.0 3.2 slice.440
  20.2 3.2 slice.439
  91.5 3.2 slice.480
  117.2 2.5 pad.144
  130.3 2.9 pad.128
  133.9 187.8 %all-gather = f32[16384,1]{0,1:T(1,128)S(1)} all-gather(f32[256,1]{0,1:T(1,128)S(1)} %slice_add_fusion.3), channel_id=2, replica_groups=mesh['tm'=64,'freq'=4] {'tm'}, dimensions={0}, use_global_device_ids=true | all-gather | bytes 66560 | tf_op jit(solution)/shard_map/all_gather | solution.py:19
  330.0 2.9 pad.146
  333.6 191.4 %all-gather.2 = f32[16384,1]{0,1:T(1,128)S(1)} all-gather(f32[256,1]{0,1:T(1,128)S(1)} %slice_add_fusion), channel_id=4, replica_groups=mesh['tm'=64,'freq'=4] {'tm'}, dimensions={0}, use_global_device_ids=true | all-gather | bytes 66560 | tf_op jit(solution)/shard_map/all_gather | solution.py:19
  527.4 186.1 %all-reduce.41 = (f32[64]{0:T(128)S(1)}, f32[64]{0:T(128)S(1)}, f32[64]{0:T(128)S(1)}, f32[64]{0:T(128)S(1)}) all-reduce(f32[64]{0:T(128)S(1)} %get-tuple-element.234, f32[64]{0:T(128)S(1)} %slice_dynamic-update-slice_fusion, f32[64]{0:T(128)S(1)} %dynamic-update-slice.2, ...), channel_id=3, replica_groups=mesh['tm'=64,'freq'=4] {'tm'}, use_global_device_ids=true, to_apply=%add.37 | all-reduce | flops 256 | bytes 2048
  713.4 5.2 while.20
  719.4 3.1 convolution_bitcast_fusion
  722.8 2.6 fusion.126
  730.0 2.4 copy.93
  733.1 342.4 %all-gather.7.cloned.1.call-done = f32[1024,768]{0,1:T(8,128)} async-done(((f32[256,768]{0,1:T(8,128)}), f32[1024,768]{0,1:T(8,128)}) %all-gather.7.cloned.1.call-update) | async-done | bytes 3145744 | tf_op jit(solution)/shard_map/all_gather | solution.py:12
  1075.4 5.1 reshape.172
  1080.6 4.6 reduce_sum.45
  1085.2 3.0 fusion.124
  1089.2 3.4 collective-permute-start
  1107.3 7.3 broadcast_multiply_fusion
  1114.6 9.1 copy.98
  1123.7 5.5 fusion.136
  1132.9 10.1 all-reduce.42
  1143.6 7.0 fusion.11
  1150.6 751.2 %all-reduce.45.cloned.1.call-done = f32[4096,256]{1,0:T(8,128)} async-done(((f32[4096,256]{1,0:T(8,128)}), f32[4096,256]{1,0:T(8,128)}) %all-reduce.45.cloned.1.call-update) | async-done | bytes 4194320 | tf_op jit(solution)/shard_map/psum | solution.py:153
  (246 shorter events, 150.3 us)
Async XLA Ops:
  7.2 1116.5 %copy-start = (bf16[256,4096]{1,0:T(8,128)(2,1)S(1)}, bf16[256,4096]{1,0:T(8,128)(2,1)}, u32[]{:S(2)}) copy-start(bf16[256,4096]{1,0:T(8,128)(2,1)} %param.19) | copy-start | bytes 6291460
  7.2 1068.2 %all-gather.7.cloned.1.call-start = ((), (), s32[]{:S(2)}) async-start(), calls=%async_computation.1 | async-start | bytes 3932160 | tf_op jit(solution)/shard_map/all_gather | solution.py:12
  9.7 3.1 copy-start.1
  15.4 79.3 %copy-start.3 = (s32[768]{0:T(1024)S(1)}, s32[768]{0:T(1024)}, u32[]{:S(2)}) copy-start(s32[768]{0:T(1024)} %param.14) | copy-start | bytes 9220
  105.5 22.8 %slice-start = ((f32[256,768]{0,1:T(8,128)}), f32[256,1]{0,1:T(1,128)S(1)}, s32[]{:S(2)}) async-start(f32[256,768]{0,1:T(8,128)} %copy-done.1), calls=%async_computation.2 | async-start | bytes 2048 | tf_op jit(solution)/shard_map/slice | solution.py:90
  113.6 209.5 %copy-start.7 = (u32[256]{0:T(256)S(1)}, u32[256]{0:T(256)}, u32[]{:S(2)}) copy-start(u32[256]{0:T(256)} %constant.229) | copy-start | bytes 3076
  113.6 212.1 %copy-start.4 = (pred[767]{0:T(1024)(128)(4,1)S(1)}, pred[767]{0:T(1024)(128)(4,1)}, u32[]{:S(2)}) copy-start(pred[767]{0:T(1024)(128)(4,1)} %get-tuple-element.180) | copy-start | bytes 2305
  113.6 213.5 %slice-start.1 = ((f32[256,768]{0,1:T(8,128)}), f32[256,1]{0,1:T(1,128)S(1)}, s32[]{:S(2)}) async-start(f32[256,768]{0,1:T(8,128)} %convert_multiply_fusion.2), calls=%async_computation.3 | async-start | bytes 2048 | tf_op jit(solution)/shard_map/slice | solution.py:90
  122.2 597.1 %copy-start.6 = (f32[256]{0:T(256)S(1)}, f32[256]{0:T(256)}, u32[]{:S(2)}) copy-start(f32[256]{0:T(256)} %param.13) | copy-start | bytes 3076
  124.1 595.2 %copy-start.2 = (bf16[256,256]{1,0:T(8,128)(2,1)S(1)}, bf16[256,256]{1,0:T(8,128)(2,1)}, u32[]{:S(2)}) copy-start(bf16[256,256]{1,0:T(8,128)(2,1)} %param.15) | copy-start | bytes 393220
  719.4 13.0 copy-start.5
  722.5 1179.3 %all-reduce.45.cloned.1.call-start = ((), (), s32[]{:S(2)}) async-start(), calls=%async_computation | async-start | bytes 8388608 | tf_op jit(solution)/shard_map/psum | solution.py:153
  1089.2 5.5 collective-permute-start
Sparse Core Ops, SparseCore 0:
  722.6 352.7 all-gather.6
  1150.7 751.0 all-reduce.44
